TPU v7x, 256 devices: a whole 4x4x8 slice. The times are simulated.
256 devices in a mesh: row: 8 (over y, core), col: 32 (over x, z).
Axes of the slice: x: 4, y: 4, z: 8, core: 2. Of those that a mesh axis runs over, the one named last changes fastest.
Arguments:
- columns: float32 [2048, 131072], P(None, ('row', 'col')), may hold values from -6000 to 6000
- seating: int32 [32], replicated, may hold values from 0 to 31, each once
Outputs:
- rotated: float32 [2048, 131072], P(None, ('row', 'col'))
All inputs are finite; a program needn't handle non-finite values.
Results may differ from a plain program's by a relative error of at most 0.0001.
Values sent between devices are 32-bit elements; how exact they have to be, the bound alone decides.
No kernel may reach another device: no remote copies, remote signals or barrier semaphores. Data moves between devices by JAX's collectives and lax.ppermute only.
A program may use at most 128 MiB of HBM per device.

v0:
```python
import jax
import jax.numpy as jnp
from jax import lax
from jax.sharding import PartitionSpec as P

BLOCK = 64
NS_STEPS = 5
highest = lax.Precision.HIGHEST


def rotation(pair_gram, total_rows):
    pair_width = pair_gram.shape[-1]
    frobenius = jnp.sqrt(jnp.sum(pair_gram * pair_gram, axis=(-2, -1), keepdims=True))
    current = pair_gram / frobenius
    identity = jnp.eye(pair_width, dtype=jnp.float32)
    inverse_root = jnp.broadcast_to(identity, pair_gram.shape)
    for newton_turn in range(NS_STEPS):
        factor = 1.5 * identity - 0.5 * jnp.matmul(inverse_root, current, precision=highest)
        current = jnp.matmul(current, factor, precision=highest)
        inverse_root = jnp.matmul(factor, inverse_root, precision=highest)
    return inverse_root * jnp.sqrt(total_rows / frobenius)


def pair_up(blocks, stride):
    count = blocks.shape[0]
    shaped = blocks.reshape(count // (2 * stride), 2, stride, blocks.shape[1], blocks.shape[2])
    return jnp.concatenate([shaped[:, 0], shaped[:, 1]], axis=2)


def split_pairs(rotated_pairs, stride):
    groups = rotated_pairs.shape[0]
    half_width = rotated_pairs.shape[2] // 2
    shaped = rotated_pairs.reshape(groups, stride, 2, half_width, rotated_pairs.shape[3])
    return jnp.transpose(shaped, (0, 2, 1, 3, 4)).reshape(
        groups * 2 * stride, half_width, rotated_pairs.shape[3]
    )


def body(columns, seating):
    block_count = seating.shape[0]
    rows_here = columns.shape[1]
    col_count = lax.axis_size("col")
    total_rows = float(rows_here * lax.axis_size("row") * col_count)
    seat_count = block_count // col_count
    seated = columns.reshape(block_count, BLOCK, rows_here)[seating].reshape(
        block_count * BLOCK, rows_here
    )
    current = seated.reshape(block_count, BLOCK, rows_here)
    for stride in (seat_count, block_count // 2):
        paired = pair_up(current, stride)
        partial_gram = jnp.einsum("gsam,gsbm->gsab", paired, paired, precision=highest)
        pair_gram = lax.psum(partial_gram, ("row", "col"))
        rotate = rotation(pair_gram, total_rows)
        moved = jnp.einsum("gsab,gsam->gsbm", rotate, paired, precision=highest)
        current = split_pairs(moved, stride)
    seated = current.reshape(block_count * BLOCK, rows_here)
    ordered = seated.reshape(block_count, BLOCK, rows_here)
    restored = jnp.zeros_like(ordered).at[seating].set(ordered)
    return restored.reshape(block_count * BLOCK, rows_here)


def solution(mesh):
    in_specs = (P(None, ("row", "col")), P())
    out_specs = P(None, ("row", "col"))
    return jax.shard_map(body, mesh=mesh, in_specs=in_specs, out_specs=out_specs, check_vma=False)
```

profile of v0, /device:TPU:2, one launch (start us, length us, event | category | flops | bytes accessed | tf_op | source)
XLA Modules:
  0.0 617.4 jit_solution(11122427788383581620)
XLA Ops:
  6.5 0.7 compare_select_fusion
  7.2 5.0 gather_fusion
  12.2 2.7 slice_bitcast_fusion.3
  15.0 1.3 copy-done
  16.3 5.0 fusion.4
  21.3 0.0 all-reduce.3.cloned.1.call-update
  21.3 0.2 all-reduce.5.cloned.1.call-start
  21.6 261.7 %all-reduce.3.cloned.1.call-done = f32[16,1,128,128]{3,2,0,1:T(8,128)} async-done(((f32[16,1,128,128]{3,2,0,1:T(8,128)}), f32[16,1,128,128]{3,2,0,1:T(8,128)}) %all-reduce.3.cloned.1.call-update) | async-done | bytes 1048592 | tf_op jit(solution)/shard_map/psum | solution.py:52
  283.3 1.5 multiply_reduce_fusion.1
  284.9 2.3 fusion.15
  287.2 1.0 fusion.25
  288.2 1.3 fusion.19
  289.5 1.2 fusion.14
  290.7 1.2 fusion.35
  291.9 1.2 fusion.34
  293.1 1.2 fusion.13
  294.3 1.2 fusion.37
  295.5 1.2 fusion.36
  296.7 1.4 fusion.12
  298.2 1.2 fusion.38
  299.4 1.2 fusion.39
  300.6 1.2 fusion.11
  301.8 1.9 convolution_multiply_fusion.6
  303.7 3.8 fusion.2
  307.5 0.5 slice_bitcast_fusion.1
  308.0 1.3 copy-done.2
  309.3 5.5 fusion.5
  314.8 0.0 all-reduce.5.cloned.1.call-update
  314.8 257.9 %all-reduce.5.cloned.1.call-done = f32[1,16,128,128]{3,2,1,0:T(8,128)} async-done(((f32[1,16,128,128]{3,2,1,0:T(8,128)}), f32[1,16,128,128]{3,2,1,0:T(8,128)}) %all-reduce.5.cloned.1.call-update) | async-done | bytes 1048592 | tf_op jit(solution)/shard_map/psum | solution.py:52
  572.8 1.5 multiply_reduce_fusion
  574.3 2.3 fusion.10
  576.7 1.0 fusion.22
  577.7 1.3 fusion.16
  579.0 1.2 fusion.9
  580.2 1.2 fusion.41
  581.4 1.2 fusion.40
  582.6 1.2 fusion.8
  583.8 1.2 fusion.43
  585.0 1.4 fusion.42
  586.3 1.2 fusion.7
  587.6 1.2 fusion.44
  588.8 1.2 fusion.45
  590.0 1.2 fusion.6
  591.2 1.9 convolution_multiply_fusion
  593.1 3.8 fusion
  596.9 2.6 copy.5
  599.5 2.5 broadcast_in_dim.4
  602.1 8.3 %scatter_fusion = f32[32,64,512]{2,1,0:T(8,128)} fusion(f32[32,64,512]{2,1,0:T(8,128)} %broadcast_in_dim.4, s32[32]{0:T(128)S(1)} %compare_select_fusion, f32[32,64,512]{2,1,0:T(8,128)} %bitcast.98), kind=kCustom, calls=%fused_computation.1 | custom fusion | bytes 12583040 | tf_op jit(solution)/shard_map/scatter | solution.py:58
  (16 shorter events, 0.1 us)
Async XLA Ops:
  6.5 276.8 %all-reduce.3.cloned.1.call-start = ((), (), s32[]{:S(2)}) async-start(), calls=%async_computation | async-start | bytes 2097152 | tf_op jit(solution)/shard_map/psum | solution.py:52
  15.0 1.3 copy-start
  21.3 551.4 %all-reduce.5.cloned.1.call-start = ((), (), s32[]{:S(2)}) async-start(), calls=%async_computation.1 | async-start | bytes 2097152 | tf_op jit(solution)/shard_map/psum | solution.py:52
  283.3 4.9 copy-start.4
  299.4 4.3 copy-start.1
  308.0 1.3 copy-start.2
  572.8 4.9 copy-start.5
  588.8 4.3 copy-start.3
Sparse Core Ops, SparseCore 0:
  21.4 261.8 all-reduce.2
  315.0 257.7 all-reduce.4
where the time goes:
time: 622 us; the launch traced here: 617 us
  waiting for transfers between devices  520 us (84%)
  matrix products  55.4 us (9%)
  local copies, waits for them, and re-layouts  24.4 us (4%)
  between operations  13.9 us (2%)
    psum x2, waiting for transfers between devices, body(): pair_gram = lax.psum(partial_gram, ('row', 'col'))  520 us
    dot_general x10, matrix products, rotation(): jnp.matmul(inverse_root, current, precision=highest)  14.6 us
    dot_general x10, matrix products, rotation(): inverse_root = jnp.matmul(factor, inverse_root, precision=highest)  13.1 us
  transfers between devices with their start and end apart: 2, of which 2 were waited for; matrix products, arithmetic and copies ran while one was open for 0% of the time, Pallas kernels for 0%

commit v1 on v0

--- a/solution.py
+++ b/solution.py
@@ -49,7 +49,7 @@
     for stride in (seat_count, block_count // 2):
         paired = pair_up(current, stride)
         partial_gram = jnp.einsum("gsam,gsbm->gsab", paired, paired, precision=highest)
-        pair_gram = lax.psum(partial_gram, ("row", "col"))
+        pair_gram = lax.psum(lax.psum(partial_gram, "col"), "row")
         rotate = rotation(pair_gram, total_rows)
         moved = jnp.einsum("gsab,gsam->gsbm", rotate, paired, precision=highest)
         current = split_pairs(moved, stride)

time: 622 us -> 540 us (0.87)
  waiting for transfers between devices: 520 us -> 438 us
    psum x2 -> x4, waiting for transfers between devices: 520 us -> 438 us  [body(): pair_gram = lax.psum(lax.psum(partial_gram, 'col'), 'row')]
  transfers between devices with their start and end apart: 2 -> 4, of which waited for: 2 -> 4; matrix products, arithmetic and copies ran while one was open for 0% -> 0% of each run, Pallas kernels for 0% -> 0%
where the time goes in v1:
time: 540 us; the launch traced here: 535 us
  waiting for transfers between devices  438 us (81%)
  matrix products  55.3 us (10%)
  local copies, waits for them, and re-layouts  24.4 us (5%)
  between operations  13.7 us (3%)
    psum x4, waiting for transfers between devices, body(): pair_gram = lax.psum(lax.psum(partial_gram, 'col'), 'row')  438 us
    dot_general x10, matrix products, rotation(): jnp.matmul(inverse_root, current, precision=highest)  15 us
    dot_general x10, matrix products, rotation(): inverse_root = jnp.matmul(factor, inverse_root, precision=highest)  13 us
  transfers between devices with their start and end apart: 4, of which 4 were waited for; matrix products, arithmetic and copies ran while one was open for 0% of the time, Pallas kernels for 0%

profile of v1, /device:TPU:2, one launch (start us, length us, event | category | flops | bytes accessed | tf_op | source)
XLA Modules:
  0.0 535.2 jit_solution(15081239934047286879)
XLA Ops:
  6.5 0.7 compare_select_fusion
  7.2 5.0 gather_fusion
  12.2 2.7 slice_bitcast_fusion.3
  15.0 1.3 copy-done
  16.3 5.0 fusion.4
  21.4 152.1 %all-reduce.5.cloned.1.call-done = f32[16,1,128,128]{3,2,0,1:T(8,128)} async-done(((f32[16,1,128,128]{3,2,0,1:T(8,128)}), f32[16,1,128,128]{3,2,0,1:T(8,128)}) %all-reduce.5.cloned.1.call-update) | async-done | bytes 1048592 | tf_op jit(solution)/shard_map/psum | solution.py:52
  173.4 0.2 all-reduce.9.cloned.1.call-start
  173.7 68.5 %all-reduce.7.cloned.1.call-done = f32[16,1,128,128]{3,2,0,1:T(8,128)} async-done(((f32[16,1,128,128]{3,2,0,1:T(8,128)}), f32[16,1,128,128]{3,2,0,1:T(8,128)}) %all-reduce.7.cloned.1.call-update) | async-done | bytes 1048592 | tf_op jit(solution)/shard_map/psum | solution.py:52
  242.2 1.5 multiply_reduce_fusion.1
  243.8 2.3 fusion.15
  246.1 1.0 fusion.25
  247.2 1.3 fusion.19
  248.4 1.2 fusion.14
  249.7 1.2 fusion.35
  250.9 1.2 fusion.34
  252.0 1.2 fusion.13
  253.3 1.2 fusion.37
  254.5 1.2 fusion.36
  255.7 1.6 fusion.12
  257.3 1.2 fusion.38
  258.5 1.2 fusion.39
  259.7 1.2 fusion.11
  260.9 1.9 convolution_multiply_fusion.6
  262.8 3.8 fusion.2
  266.6 0.5 slice_bitcast_fusion.1
  267.1 1.3 copy-done.2
  268.4 5.2 fusion.5
  273.7 148.4 %all-reduce.9.cloned.1.call-done = f32[1,16,128,128]{3,2,1,0:T(8,128)} async-done(((f32[1,16,128,128]{3,2,1,0:T(8,128)}), f32[1,16,128,128]{3,2,1,0:T(8,128)}) %all-reduce.9.cloned.1.call-update) | async-done | bytes 1048592 | tf_op jit(solution)/shard_map/psum | solution.py:52
  422.2 68.7 %all-reduce.11.cloned.1.call-done = f32[1,16,128,128]{3,2,1,0:T(8,128)} async-done(((f32[1,16,128,128]{3,2,1,0:T(8,128)}), f32[1,16,128,128]{3,2,1,0:T(8,128)}) %all-reduce.11.cloned.1.call-update) | async-done | bytes 1048592 | tf_op jit(solution)/shard_map/psum | solution.py:52
  490.9 1.5 multiply_reduce_fusion
  492.4 2.3 fusion.10
  494.8 1.0 fusion.22
  495.8 1.3 fusion.16
  497.1 1.2 fusion.9
  498.3 1.2 fusion.41
  499.5 1.2 fusion.40
  500.7 1.2 fusion.8
  501.9 1.2 fusion.43
  503.1 1.2 fusion.42
  504.3 1.4 fusion.7
  505.7 1.2 fusion.44
  506.9 1.2 fusion.45
  508.1 1.2 fusion.6
  509.3 1.9 convolution_multiply_fusion
  511.3 3.8 fusion
  515.0 2.6 copy.5
  517.7 2.5 broadcast_in_dim.4
  520.2 8.3 %scatter_fusion = f32[32,64,512]{2,1,0:T(8,128)} fusion(f32[32,64,512]{2,1,0:T(8,128)} %broadcast_in_dim.4, s32[32]{0:T(128)S(1)} %compare_select_fusion, f32[32,64,512]{2,1,0:T(8,128)} %bitcast.98), kind=kCustom, calls=%fused_computation.1 | custom fusion | bytes 12583040 | tf_op jit(solution)/shard_map/scatter | solution.py:58
  (22 shorter events, 0.2 us)
Async XLA Ops:
  6.5 166.9 %all-reduce.5.cloned.1.call-start = ((), (), s32[]{:S(2)}) async-start(), calls=%async_computation | async-start | bytes 2097152 | tf_op jit(solution)/shard_map/psum | solution.py:52
  15.0 1.3 copy-start
  21.3 220.9 %all-reduce.7.cloned.1.call-start = ((), (), s32[]{:S(2)}) async-start(), calls=%async_computation.1 | async-start | bytes 2097152 | tf_op jit(solution)/shard_map/psum | solution.py:52
  173.4 248.7 %all-reduce.9.cloned.1.call-start = ((), (), s32[]{:S(2)}) async-start(), calls=%async_computation.2 | async-start | bytes 2097152 | tf_op jit(solution)/shard_map/psum | solution.py:52
  242.2 4.9 copy-start.4
  258.5 4.3 copy-start.1
  267.1 1.3 copy-start.2
  273.7 217.2 %all-reduce.11.cloned.1.call-start = ((), (), s32[]{:S(2)}) async-start(), calls=%async_computation.3 | async-start | bytes 2097152 | tf_op jit(solution)/shard_map/psum | solution.py:52
  490.9 4.9 copy-start.5
  506.9 4.3 copy-start.3
Sparse Core Ops, SparseCore 0:
  21.4 151.9 all-reduce.4
  175.8 66.4 all-reduce.6
  273.8 148.3 all-reduce.8
  424.4 66.4 all-reduce.10
